TPU v7x, 512 devices: a whole 4x4x16 slice. The times are simulated.
512 devices in a mesh: rows: 16 (over z_lo, x), cols: 32 (over y, z_hi, core).
Axes of the slice: x: 4, y: 4, z: 16 (z_hi: 4, z_lo: 4; z = z_hi * 4 + z_lo), core: 2. Of those that a mesh axis runs over, the one named last changes fastest.
Arguments:
- file_pixels: bfloat16 [48, 512, 4096], P(None, ('rows', 'cols')), may hold values from -6 to 6
- patchify_weight: bfloat16 [64, 48], replicated, may hold values from -0.875 to 0.875
- patchify_bias: float32 [64], replicated, may hold values from -3 to 3
- norm_gain: float32 [64], replicated, may hold values from 0.5 to 1.5
- norm_offset_vector: float32 [64], replicated, may hold values from -3 to 3
- kernel: float32 [64, 49], replicated, may hold values from -0.875 to 0.875
- kernel_offset: float32 [64], replicated, may hold values from -3 to 3
- cotangent: bfloat16 [64, 512, 4096], P(None, 'rows', 'cols'), may hold values from -10 to 10, as said below
Outputs:
- stem_output: bfloat16 [64, 512, 4096], P(None, 'rows', 'cols')
- weight_grad: float32 [64, 48], replicated
- bias_grad: float32 [64], replicated
- norm_scale_gradient: float32 [64], replicated
- shift_grad: float32 [64], replicated
- kernel_grad: float32 [64, 49], replicated
- offset_grad: float32 [64], replicated
Inputs may be any that keep to these rules, and one draw needn't show every extreme that they name: A cotangent of order one.
All inputs are finite; a program needn't handle non-finite values.
Results may differ from a plain program's by a relative error of at most 0.0055.
Values may be sent and summed in bfloat16 or wider, within the bound.
A program may use at most 64 MiB of HBM per device.

v0:
```python
import math
import jax
import jax.numpy as jnp
from jax import lax
from jax.sharding import PartitionSpec as P

norm_eps = 1e-06
side = 7


def extended(block, sides, width):
    for axis, dim in sides:
        count = lax.axis_size(axis)
        forward = [(i, i + 1) for i in range(count - 1)]
        backward = [(target, source) for source, target in forward]
        low = lax.ppermute(
            lax.slice_in_dim(block, block.shape[dim] - width, None, axis=dim), axis, forward
        )
        high = lax.ppermute(lax.slice_in_dim(block, 0, width, axis=dim), axis, backward)
        block = jnp.concatenate([low, block, high], axis=dim)
    return block


def embed_patches(pixel_values, weight, bias):
    flat = pixel_values.reshape(pixel_values.shape[0], -1)
    mixed = jnp.dot(weight, flat, preferred_element_type=jnp.float32) + bias[:, None]
    return mixed.astype(jnp.bfloat16).reshape(
        weight.shape[0], pixel_values.shape[1], pixel_values.shape[2]
    )


def apply_layer_norm(patch_embedding):
    values = patch_embedding.astype(jnp.float32)
    center = values - jnp.mean(values, axis=0, keepdims=True)
    spread = jnp.mean(center * center, axis=0, keepdims=True)
    inverse_deviation = lax.rsqrt(spread + norm_eps)
    return (center * inverse_deviation, inverse_deviation)


def depthwise(padded, taps, height, breadth):
    total = jnp.zeros((padded.shape[0], height, breadth), jnp.float32)
    for tap_row in range(side):
        for tap_col in range(side):
            window = padded[:, tap_row : tap_row + height, tap_col : tap_col + breadth].astype(
                jnp.float32
            )
            total = total + taps[:, tap_row * side + tap_col][:, None, None] * window
    return total


def kernel_terms(padded, upstream, height, breadth):
    terms = []
    for tap_row in range(side):
        for tap_col in range(side):
            window = padded[:, tap_row : tap_row + height, tap_col : tap_col + breadth].astype(
                jnp.float32
            )
            terms.append(jnp.sum(window * upstream, axis=(1, 2)))
    return jnp.stack(terms, axis=1)


def per_device(
    file_pixels,
    patchify_weight,
    patchify_bias,
    norm_gain,
    norm_offset_vector,
    kernel,
    kernel_offset,
    cotangent,
):
    height = cotangent.shape[1]
    breadth = cotangent.shape[2]
    factor = 1.0 / math.sqrt(height * lax.axis_size("rows") * breadth * lax.axis_size("cols"))
    patch_embedding = lax.all_to_all(
        embed_patches(file_pixels, patchify_weight, patchify_bias),
        "cols",
        split_axis=2,
        concat_axis=1,
        tiled=True,
    )
    centered_input, inverse_deviation = apply_layer_norm(patch_embedding)
    scale_factor = norm_gain[:, None, None]
    normalized_output = (centered_input * scale_factor + norm_offset_vector[:, None, None]).astype(
        jnp.bfloat16
    )
    tall = extended(normalized_output, (("rows", 1),), 3)
    padded = extended(tall, (("cols", 2),), 3)
    cot_tall = extended(cotangent, (("rows", 1),), 3)
    cot_pad = extended(cot_tall, (("cols", 2),), 3)
    stem_output = (
        depthwise(padded, kernel, height, breadth) + kernel_offset[:, None, None]
    ).astype(jnp.bfloat16)
    upstream = cotangent.astype(jnp.float32) * factor
    kernel_grad = kernel_terms(padded, upstream, height, breadth)
    offset_grad = jnp.sum(upstream, axis=(1, 2))
    normalized_gradient = depthwise(cot_pad, kernel[:, ::-1], height, breadth) * factor
    norm_scale_gradient = jnp.sum(normalized_gradient * centered_input, axis=(1, 2))
    shift_grad = jnp.sum(normalized_gradient, axis=(1, 2))
    input_gradient = normalized_gradient * scale_factor
    patch_gradient = inverse_deviation * (
        input_gradient
        - jnp.mean(input_gradient, axis=0, keepdims=True)
        - centered_input * jnp.mean(input_gradient * centered_input, axis=0, keepdims=True)
    )
    patch_gradient = patch_gradient.astype(jnp.bfloat16)
    local_grad = lax.all_to_all(patch_gradient, "cols", split_axis=1, concat_axis=2, tiled=True)
    partial_weight = lax.dot_general(
        local_grad.reshape(local_grad.shape[0], -1),
        file_pixels.reshape(file_pixels.shape[0], -1),
        (((1,), (1,)), ((), ())),
        preferred_element_type=jnp.float32,
    )
    bias_part = jnp.sum(local_grad.astype(jnp.float32), axis=(1, 2))
    totals = lax.psum(
        (partial_weight, bias_part, norm_scale_gradient, shift_grad, kernel_grad, offset_grad),
        ("rows", "cols"),
    )
    return (stem_output, totals[0], totals[1], totals[2], totals[3], totals[4], totals[5])


def solution(mesh):
    return jax.shard_map(
        per_device,
        mesh=mesh,
        in_specs=(
            P(None, ("rows", "cols"), None),
            P(),
            P(),
            P(),
            P(),
            P(),
            P(),
            P(None, "rows", "cols"),
        ),
        out_specs=(P(None, "rows", "cols"), P(), P(), P(), P(), P(), P()),
        check_vma=False,
    )
```

profile of v0, /device:TPU:1, one launch (start us, length us, event | category | flops | bytes accessed | tf_op | source)
XLA Modules:
  0.0 420.4 jit_solution(11450217107587844098)
XLA Ops:
  0.6 0.0 copy-start
  0.6 1.0 copy-done
  1.6 1.0 fusion.1
  2.7 2.8 copy.94
  5.5 0.5 broadcast.111
  6.0 22.4 %reduce.3 = bf16[4096,64]{1,0:T(8,128)(2,1)S(1)} reduce(bf16[4096,1,64]{2,1,0:T(2,128)(2,1)S(1)} %bitcast.174, bf16[]{:T(256)} %broadcast.111), dimensions={1}, to_apply=%bitcast.163.reduce_sub_computation | reduce | bytes 1048578
  28.4 1.5 reshape.173
  29.9 19.6 %all-to-all-start = ((bf16[32,2,4096]{2,1,0:T(2,128)(2,1)}), bf16[32,2,4096]{2,1,0:T(2,128)(2,1)}, u32[]{:S(2)}, u32[]{:S(2)}) async-start(bf16[32,2,4096]{2,1,0:T(2,128)(2,1)} %reshape.173), calls=%async_computation | async-start | bytes 1048576 | tf_op jit(solution)/shard_map/all_to_all | solution.py:75
  49.5 1.7 copy.98
  51.2 0.1 fusion.190
  51.4 3.1 collective-permute-start.4
  54.5 1.3 collective-permute-start.5
  55.8 0.5 slice_bitcast_fusion.48
  56.3 0.7 slice_bitcast_fusion.47
  57.0 0.6 slice_bitcast_fusion.46
  57.6 3.3 collective-permute-done.5
  61.0 8.4 %collective-permute-start.6 = (bf16[64,38,3]{0,1,2:T(8,128)(2,1)S(1)}, bf16[64,38,3]{0,1,2:T(8,128)(2,1)S(1)}, u32[]{:S(2)}, u32[]{:S(2)}) collective-permute-start(bf16[64,38,3]{0,1,2:T(8,128)(2,1)S(1)} %get-tuple-element.117), channel_id=1, source_target_pairs={{0,1},{1,2},{2,3},{3,4},{4,5},{5,6},{6,7},{7,8},{8,9},{9,10},{10,1... | collective-permute-start | bytes 43784 | tf_op jit(solution)/shard_map/ppermute | solution.py:16
  69.4 13.0 %collective-permute-start.7 = (bf16[64,38,3]{0,1,2:T(8,128)(2,1)S(1)}, bf16[64,38,3]{0,1,2:T(8,128)(2,1)S(1)}, u32[]{:S(2)}, u32[]{:S(2)}) collective-permute-start(bf16[64,38,3]{0,1,2:T(8,128)(2,1)S(1)} %get-tuple-element.118), channel_id=1, source_target_pairs={{1,0},{2,1},{3,2},{4,3},{5,4},{6,5},{7,6},{8,7},{9,8},{10,9},{11,1... | collective-permute-start | bytes 43784 | tf_op jit(solution)/shard_map/ppermute | solution.py:19
  82.4 0.5 broadcast_multiply_fusion.3
  83.0 3.8 maximum_maximum_fusion.1
  86.8 5.5 %reshape.174 = bf16[4096,1,64]{2,1,0:T(2,128)(2,1)} reshape(bf16[32,2,4096]{2,1,0:T(2,128)(2,1)} %all-to-all-done) | data formatting | bytes 1048576
  92.3 31.6 %convert_reduce_fusion.1 = f32[4096]{0:T(1024)S(1)} fusion(bf16[4096,1,64]{2,1,0:T(2,128)(2,1)} %reshape.174), kind=kLoop, calls=%fused_computation.334 | loop fusion | flops 520192 | bytes 540672 | tf_op jit(solution)/shard_map/reduce_sum | solution.py:34
  124.0 3.3 bitcast_convert_fusion
  127.2 58.9 %multiply_reduce_fusion.2 = f32[4096]{0:T(1024)S(1)} fusion(f32[4096]{0:T(1024)S(1)} %get-tuple-element.177, bf16[4096,1,64]{2,1,0:T(2,128)(2,1)S(1)} %copy-done.3), kind=kLoop, calls=%fused_computation.233 | loop fusion | flops 1044480 | bytes 557056 | tf_op jit(solution)/shard_map/reduce_sum | solution.py:35
  186.1 0.1 copy.97
  186.2 0.1 copy.95
  186.4 22.9 %multiply_reduce_fusion = (f32[64]{0:T(128)}, f32[32,128]{0,1:T(8,128)S(1)}, f32[32,128]{0,1:T(8,128)S(1)}, f32[64]{0:T(128)}, f32[64,32,128]{0,1,2:T(8,128)S(1)}) fusion(f32[32,128]{0,1:T(8,128)S(1)} %copy.97, f32[32,128]{0,1:T(8,128)S(1)} %copy.95, f32[64,32,128]{0,2,1:T(8,128)} %bitcast.172, f32[64]{0:T(128)} %broadcast_multiply_fusion.3, ...), kind=kLoop, calls=%fused_computation.228 | loop fusion | flops 45604736 | bytes 24818688 | tf_op jit(solution)/shard_map/reduce_sum | solution.py:98
  209.3 3.5 multiply_convert_fusion
  212.8 0.1 fusion.191
  212.9 3.1 collective-permute-start
  216.1 1.3 collective-permute-start.1
  217.4 0.6 collective-permute-done
  218.0 3.8 collective-permute-done.1
  221.8 9.0 %collective-permute-start.2 = (bf16[64,38,3]{0,1,2:T(8,128)(2,1)S(1)}, bf16[64,38,3]{0,1,2:T(8,128)(2,1)S(1)}, u32[]{:S(2)}, u32[]{:S(2)}) collective-permute-start(bf16[64,38,3]{0,1,2:T(8,128)(2,1)S(1)} %get-tuple-element.121), channel_id=1, source_target_pairs={{0,1},{1,2},{2,3},{3,4},{4,5},{5,6},{6,7},{7,8},{8,9},{9,10},{10,1... | collective-permute-start | bytes 43784 | tf_op jit(solution)/shard_map/ppermute | solution.py:16
  230.8 1.9 collective-permute-start.3
  232.7 1.9 copy.104
  234.6 14.7 %all-to-all-start.1 = ((bf16[64,32,128]{2,0,1:T(8,128)(2,1)}), bf16[64,32,128]{2,0,1:T(8,128)(2,1)S(1)}, u32[]{:S(2)}, u32[]{:S(2)}) async-start(bf16[64,32,128]{2,0,1:T(8,128)(2,1)} %copy.104), calls=%async_computation.1 | async-start | bytes 1048576 | tf_op jit(solution)/shard_map/all_to_all | solution.py:107
  249.4 4.1 maximum_maximum_fusion
  253.9 7.2 %fusion.148 = (f32[64]{0:T(128)}, f32[64]{0:T(128)}, f32[64]{0:T(128)}, f32[64]{0:T(128)}, f32[64]{0:T(128)}, /*index=5*/f32[64]{0:T(128)}, f32[64]{0:T(128)}, f...) fusion(bf16[64,32,128]{0,1,2:T(8,128)(2,1)S(1)} %copy-done.2, ...), kind=kLoop, calls=%fused_computation.200 | loop fusion | flops 14678912 | bytes 9966080 | tf_op jit(solution)/shard_map/reduce_sum | solution.py:58
  261.5 17.8 %add_convert_fusion = bf16[64,32,128]{0,1,2:T(8,128)(2,1)} fusion(bf16[64,32,128]{0,1,2:T(8,128)(2,1)S(1)} %copy-done.5, bf16[64,3,128]{0,1,2:T(4,128)(2,1)S(1)} %copy-done.8, bf16[64,3,128]{0,1,2:T(4,128)(2,1)S(1)} %collective-permute-done, f32[64]{0:T(128)} %param.14, f32[64]{0:T(128)S(1)} %copy-done.50, f32[64]{0:T(128)S(1)} %copy-done.51, ...), kind=kLoop, calls=%fused_computation.231 | loop fusion | flops 43515904 | bytes 23179776 | tf_op jit(solution)/shard_map/convert_element_type | solution.py:93
  279.3 4.6 %fusion.147 = (f32[64]{0:T(128)S(1)}, f32[64]{0:T(128)S(1)}, f32[64]{0:T(128)S(1)}, f32[64]{0:T(128)S(1)}, f32[64]{0:T(128)S(1)}, /*index=5*/f32[64]{0:T(128)S(1...) fusion(bf16[64,32,128]{0,1,2:T(8,128)(2,1)S(1)} %copy-done.2, ...), kind=kLoop, calls=%fused_computation.199 | loop fusion | flops 13106560 | bytes 2722304 | tf_op jit(solution)/shard_map/reduce_sum | solution.py:58
  283.9 3.6 copy.106
  287.5 0.8 fusion.102
  288.5 6.8 %fusion.144 = (f32[64]{0:T(128)S(1)}, f32[64]{0:T(128)S(1)}, f32[64]{0:T(128)S(1)}, f32[64]{0:T(128)S(1)}, f32[64]{0:T(128)S(1)}, /*index=5*/f32[64]{0:T(128)S(1...) fusion(bf16[64,32,128]{0,1,2:T(8,128)(2,1)S(1)} %copy-done.2, ...), kind=kLoop, calls=%fused_computation.196 | loop fusion | flops 14940992 | bytes 9966336 | tf_op jit(solution)/shard_map/reduce_sum | solution.py:58
  295.5 0.1 stack.199
  295.7 0.2 convert_reduce_fusion
  295.8 0.3 fusion.183
  296.1 123.9 %all-reduce = (f32[64,48]{0,1:T(8,128)}, f32[64]{0:T(128)}, f32[64]{0:T(128)}, f32[64]{0:T(128)}, f32[64,49]{0,1:T(8,128)}, /*index=5*/f32[64]{0:T(128)}) all-reduce(f32[64,48]{0,1:T(8,128)S(1)} %fusion.183, f32[64]{0:T(128)S(1)} %convert_reduce_fusion, f32[64]{0:T(128)S(1)} %copy-done.70, ...), channel_id=1, replica_groups=mesh['rows'=16,'cols'=32] {'rows','cols'}, use_global_device_ids=true, to_apply=%region_4.0 | all-reduce | flops 6464 | bytes 51712 | tf_op jit(solution)/shard_map/psum | solution.py:115
  (162 shorter events, 0.4 us)
Async XLA Ops:
  28.4 21.1 %copy-start.9 = (bf16[64,32,128]{2,1,0:T(8,128)(2,1)S(1)}, bf16[64,32,128]{2,1,0:T(8,128)(2,1)}, u32[]{:S(2)}) copy-start(bf16[64,32,128]{2,1,0:T(8,128)(2,1)} %param.15) | copy-start | bytes 1572868
  28.4 27.4 %copy-start.10 = (f32[64,49]{0,1:T(8,128)S(1)}, f32[64,49]{0,1:T(8,128)}, u32[]{:S(2)}) copy-start(f32[64,49]{0,1:T(8,128)} %param.13) | copy-start | bytes 37636
  29.9 52.5 %copy-start.73 = (f32[64]{0:T(128)S(1)}, f32[64]{0:T(128)}, u32[]{:S(2)}) copy-start(f32[64]{0:T(128)} %param.11) | copy-start | bytes 772
  29.9 56.8 %all-to-all-start = ((bf16[32,2,4096]{2,1,0:T(2,128)(2,1)}), bf16[32,2,4096]{2,1,0:T(2,128)(2,1)}, u32[]{:S(2)}, u32[]{:S(2)}) async-start(bf16[32,2,4096]{2,1,0:T(2,128)(2,1)} %reshape.173), calls=%async_computation | async-start | bytes 1048576 | tf_op jit(solution)/shard_map/all_to_all | solution.py:75
  51.2 31.7 %copy-start.1 = (bf16[64,32,128]{0,1,2:T(8,128)(2,1)}, bf16[64,32,128]{0,1,2:T(8,128)(2,1)S(1)}, u32[]{:S(2)}) copy-start(bf16[64,32,128]{0,1,2:T(8,128)(2,1)S(1)} %copy.98) | copy-start | bytes 1572868
  51.4 6.3 %collective-permute-start.4 = (bf16[64,3,128]{0,1,2:T(4,128)(2,1)S(1)}, bf16[64,3,128]{0,1,2:T(4,128)(2,1)S(1)}, u32[]{:S(2)}, u32[]{:S(2)}) collective-permute-start(bf16[64,3,128]{0,1,2:T(4,128)(2,1)S(1)} %get-tuple-element.123), channel_id=1, source_target_pairs={{0,32},{32,64},{64,96},{96,128},{128,160},{160,192},{192,224},{224... | collective-permute-start | bytes 147464 | tf_op jit(solution)/shard_map/ppermute | solution.py:16
  54.5 6.5 %collective-permute-start.5 = (bf16[64,3,128]{0,1,2:T(4,128)(2,1)S(1)}, bf16[64,3,128]{0,1,2:T(4,128)(2,1)S(1)}, u32[]{:S(2)}, u32[]{:S(2)}) collective-permute-start(bf16[64,3,128]{0,1,2:T(4,128)(2,1)S(1)} %get-tuple-element.124), channel_id=1, source_target_pairs={{32,0},{64,32},{96,64},{128,96},{160,128},{192,160},{224,192},{256... | collective-permute-start | bytes 147464 | tf_op jit(solution)/shard_map/ppermute | solution.py:19
  56.3 130.0 %copy-start.11 = (f32[64]{0:T(128)}, f32[64]{0:T(128)S(1)}, u32[]{:S(2)}) copy-start(f32[64]{0:T(128)S(1)} %get-tuple-element.139) | copy-start | bytes 772
  56.3 130.0 %copy-start.13 = (f32[64]{0:T(128)}, f32[64]{0:T(128)S(1)}, u32[]{:S(2)}) copy-start(f32[64]{0:T(128)S(1)} %get-tuple-element.140) | copy-start | bytes 772
  56.3 130.0 %copy-start.15 = (f32[64]{0:T(128)}, f32[64]{0:T(128)S(1)}, u32[]{:S(2)}) copy-start(f32[64]{0:T(128)S(1)} %get-tuple-element.141) | copy-start | bytes 772
  56.3 130.0 %copy-start.17 = (f32[64]{0:T(128)}, f32[64]{0:T(128)S(1)}, u32[]{:S(2)}) copy-start(f32[64]{0:T(128)S(1)} %get-tuple-element.142) | copy-start | bytes 772
  61.0 22.0 %collective-permute-start.6 = (bf16[64,38,3]{0,1,2:T(8,128)(2,1)S(1)}, bf16[64,38,3]{0,1,2:T(8,128)(2,1)S(1)}, u32[]{:S(2)}, u32[]{:S(2)}) collective-permute-start(bf16[64,38,3]{0,1,2:T(8,128)(2,1)S(1)} %get-tuple-element.117), channel_id=1, source_target_pairs={{0,1},{1,2},{2,3},{3,4},{4,5},{5,6},{6,7},{7,8},{8,9},{9,10},{10,1... | collective-permute-start | bytes 43784 | tf_op jit(solution)/shard_map/ppermute | solution.py:16
  69.4 13.5 %collective-permute-start.7 = (bf16[64,38,3]{0,1,2:T(8,128)(2,1)S(1)}, bf16[64,38,3]{0,1,2:T(8,128)(2,1)S(1)}, u32[]{:S(2)}, u32[]{:S(2)}) collective-permute-start(bf16[64,38,3]{0,1,2:T(8,128)(2,1)S(1)} %get-tuple-element.118), channel_id=1, source_target_pairs={{1,0},{2,1},{3,2},{4,3},{5,4},{6,5},{7,6},{8,7},{9,8},{10,9},{11,1... | collective-permute-start | bytes 43784 | tf_op jit(solution)/shard_map/ppermute | solution.py:19
  92.3 31.7 %copy-start.3 = (bf16[4096,1,64]{2,1,0:T(2,128)(2,1)S(1)}, bf16[4096,1,64]{2,1,0:T(2,128)(2,1)}, u32[]{:S(2)}) copy-start(bf16[4096,1,64]{2,1,0:T(2,128)(2,1)} %reshape.174) | copy-start | bytes 1572868
  186.4 22.9 %copy-start.6 = (f32[64,1,4096]{0,1,2:T(1,128)S(1)}, f32[64,1,4096]{0,1,2:T(1,128)}, u32[]{:S(2)}) copy-start(f32[64,1,4096]{0,1,2:T(1,128)} %bitcast_convert_fusion) | copy-start | bytes 3145732
  186.4 22.9 %copy-start.72 = (f32[64]{0:T(128)S(1)}, f32[64]{0:T(128)}, u32[]{:S(2)}) copy-start(f32[64]{0:T(128)} %broadcast_multiply_fusion.3) | copy-start | bytes 772
  186.4 22.9 %copy-start.74 = (f32[64]{0:T(128)S(1)}, f32[64]{0:T(128)}, u32[]{:S(2)}) copy-start(f32[64]{0:T(128)} %param.11) | copy-start | bytes 772
  186.4 22.9 %copy-start.75 = (f32[64]{0:T(128)S(1)}, f32[64]{0:T(128)}, u32[]{:S(2)}) copy-start(f32[64]{0:T(128)} %param.12) | copy-start | bytes 772
  212.8 9.0 %copy-start.4 = (bf16[64,32,128]{0,1,2:T(8,128)(2,1)}, bf16[64,32,128]{0,1,2:T(8,128)(2,1)S(1)}, u32[]{:S(2)}) copy-start(bf16[64,32,128]{0,1,2:T(8,128)(2,1)S(1)} %get-tuple-element.114) | copy-start | bytes 1572868
  212.9 5.1 %collective-permute-start = (bf16[64,3,128]{0,1,2:T(4,128)(2,1)S(1)}, bf16[64,3,128]{0,1,2:T(4,128)(2,1)S(1)}, u32[]{:S(2)}, u32[]{:S(2)}) collective-permute-start(bf16[64,3,128]{0,1,2:T(4,128)(2,1)S(1)} %get-tuple-element.125), channel_id=1, source_target_pairs={{0,32},{32,64},{64,96},{96,128},{128,160},{160,192},{192,224},{224... | collective-permute-start | bytes 147464 | tf_op jit(solution)/shard_map/ppermute | solution.py:16
  216.1 5.7 %collective-permute-start.1 = (bf16[64,3,128]{0,1,2:T(4,128)(2,1)S(1)}, bf16[64,3,128]{0,1,2:T(4,128)(2,1)S(1)}, u32[]{:S(2)}, u32[]{:S(2)}) collective-permute-start(bf16[64,3,128]{0,1,2:T(4,128)(2,1)S(1)} %get-tuple-element.126), channel_id=1, source_target_pairs={{32,0},{64,32},{96,64},{128,96},{160,128},{192,160},{224,192},{256... | collective-permute-start | bytes 147464 | tf_op jit(solution)/shard_map/ppermute | solution.py:19
  221.8 27.6 %copy-start.7 = (bf16[64,3,128]{0,1,2:T(4,128)(2,1)}, bf16[64,3,128]{0,1,2:T(4,128)(2,1)S(1)}, u32[]{:S(2)}) copy-start(bf16[64,3,128]{0,1,2:T(4,128)(2,1)S(1)} %collective-permute-done.1) | copy-start | bytes 147460
  221.8 27.5 %collective-permute-start.2 = (bf16[64,38,3]{0,1,2:T(8,128)(2,1)S(1)}, bf16[64,38,3]{0,1,2:T(8,128)(2,1)S(1)}, u32[]{:S(2)}, u32[]{:S(2)}) collective-permute-start(bf16[64,38,3]{0,1,2:T(8,128)(2,1)S(1)} %get-tuple-element.121), channel_id=1, source_target_pairs={{0,1},{1,2},{2,3},{3,4},{4,5},{5,6},{6,7},{7,8},{8,9},{9,10},{10,1... | collective-permute-start | bytes 43784 | tf_op jit(solution)/shard_map/ppermute | solution.py:16
  230.8 18.6 %collective-permute-start.3 = (bf16[64,38,3]{0,1,2:T(8,128)(2,1)S(1)}, bf16[64,38,3]{0,1,2:T(8,128)(2,1)S(1)}, u32[]{:S(2)}, u32[]{:S(2)}) collective-permute-start(bf16[64,38,3]{0,1,2:T(8,128)(2,1)S(1)} %get-tuple-element.122), channel_id=1, source_target_pairs={{1,0},{2,1},{3,2},{4,3},{5,4},{6,5},{7,6},{8,7},{9,8},{10,9},{11,1... | collective-permute-start | bytes 43784 | tf_op jit(solution)/shard_map/ppermute | solution.py:19
  234.6 61.0 %all-to-all-start.1 = ((bf16[64,32,128]{2,0,1:T(8,128)(2,1)}), bf16[64,32,128]{2,0,1:T(8,128)(2,1)S(1)}, u32[]{:S(2)}, u32[]{:S(2)}) async-start(bf16[64,32,128]{2,0,1:T(8,128)(2,1)} %copy.104), calls=%async_computation.1 | async-start | bytes 1048576 | tf_op jit(solution)/shard_map/all_to_all | solution.py:107
  253.5 7.6 %copy-start.5 = (bf16[64,32,128]{0,1,2:T(8,128)(2,1)S(1)}, bf16[64,32,128]{0,1,2:T(8,128)(2,1)}, u32[]{:S(2)}) copy-start(bf16[64,32,128]{0,1,2:T(8,128)(2,1)} %copy-done.4) | copy-start | bytes 1572868
  253.5 7.6 %copy-start.8 = (bf16[64,3,128]{0,1,2:T(4,128)(2,1)S(1)}, bf16[64,3,128]{0,1,2:T(4,128)(2,1)}, u32[]{:S(2)}) copy-start(bf16[64,3,128]{0,1,2:T(4,128)(2,1)} %copy-done.7) | copy-start | bytes 147460
  253.5 7.6 %copy-start.12 = (f32[64]{0:T(128)S(1)}, f32[64]{0:T(128)}, u32[]{:S(2)}) copy-start(f32[64]{0:T(128)} %copy-done.11) | copy-start | bytes 772
  253.5 7.6 %copy-start.14 = (f32[64]{0:T(128)S(1)}, f32[64]{0:T(128)}, u32[]{:S(2)}) copy-start(f32[64]{0:T(128)} %copy-done.13) | copy-start | bytes 772
  253.5 7.6 %copy-start.16 = (f32[64]{0:T(128)S(1)}, f32[64]{0:T(128)}, u32[]{:S(2)}) copy-start(f32[64]{0:T(128)} %copy-done.15) | copy-start | bytes 772
  253.6 7.6 %copy-start.18 = (f32[64]{0:T(128)S(1)}, f32[64]{0:T(128)}, u32[]{:S(2)}) copy-start(f32[64]{0:T(128)} %copy-done.17) | copy-start | bytes 772
  253.6 7.6 %copy-start.19 = (f32[64]{0:T(128)S(1)}, f32[64]{0:T(128)}, u32[]{:S(2)}) copy-start(f32[64]{0:T(128)} %get-tuple-element.143) | copy-start | bytes 772
  253.6 7.6 %copy-start.20 = (f32[64]{0:T(128)S(1)}, f32[64]{0:T(128)}, u32[]{:S(2)}) copy-start(f32[64]{0:T(128)} %get-tuple-element.144) | copy-start | bytes 772
  253.6 7.6 %copy-start.21 = (f32[64]{0:T(128)S(1)}, f32[64]{0:T(128)}, u32[]{:S(2)}) copy-start(f32[64]{0:T(128)} %get-tuple-element.145) | copy-start | bytes 772
  253.6 7.6 %copy-start.22 = (f32[64]{0:T(128)S(1)}, f32[64]{0:T(128)}, u32[]{:S(2)}) copy-start(f32[64]{0:T(128)} %get-tuple-element.146) | copy-start | bytes 772
  253.6 7.6 %copy-start.23 = (f32[64]{0:T(128)S(1)}, f32[64]{0:T(128)}, u32[]{:S(2)}) copy-start(f32[64]{0:T(128)} %get-tuple-element.147) | copy-start | bytes 772
  253.6 7.6 %copy-start.24 = (f32[64]{0:T(128)S(1)}, f32[64]{0:T(128)}, u32[]{:S(2)}) copy-start(f32[64]{0:T(128)} %get-tuple-element.148) | copy-start | bytes 772
  253.6 7.6 %copy-start.25 = (f32[64]{0:T(128)S(1)}, f32[64]{0:T(128)}, u32[]{:S(2)}) copy-start(f32[64]{0:T(128)} %get-tuple-element.149) | copy-start | bytes 772
  253.6 7.6 %copy-start.26 = (f32[64]{0:T(128)S(1)}, f32[64]{0:T(128)}, u32[]{:S(2)}) copy-start(f32[64]{0:T(128)} %get-tuple-element.150) | copy-start | bytes 772
  253.7 7.6 %copy-start.27 = (f32[64]{0:T(128)S(1)}, f32[64]{0:T(128)}, u32[]{:S(2)}) copy-start(f32[64]{0:T(128)} %get-tuple-element.151) | copy-start | bytes 772
  253.7 7.6 %copy-start.28 = (f32[64]{0:T(128)S(1)}, f32[64]{0:T(128)}, u32[]{:S(2)}) copy-start(f32[64]{0:T(128)} %get-tuple-element.152) | copy-start | bytes 772
  253.7 7.6 %copy-start.29 = (f32[64]{0:T(128)S(1)}, f32[64]{0:T(128)}, u32[]{:S(2)}) copy-start(f32[64]{0:T(128)} %get-tuple-element.153) | copy-start | bytes 772
  253.7 7.6 %copy-start.30 = (f32[64]{0:T(128)S(1)}, f32[64]{0:T(128)}, u32[]{:S(2)}) copy-start(f32[64]{0:T(128)} %get-tuple-element.154) | copy-start | bytes 772
  253.7 7.6 %copy-start.31 = (f32[64]{0:T(128)S(1)}, f32[64]{0:T(128)}, u32[]{:S(2)}) copy-start(f32[64]{0:T(128)} %get-tuple-element.155) | copy-start | bytes 772
  253.7 7.6 %copy-start.32 = (f32[64]{0:T(128)S(1)}, f32[64]{0:T(128)}, u32[]{:S(2)}) copy-start(f32[64]{0:T(128)} %get-tuple-element.156) | copy-start | bytes 772
  253.7 7.6 %copy-start.33 = (f32[64]{0:T(128)S(1)}, f32[64]{0:T(128)}, u32[]{:S(2)}) copy-start(f32[64]{0:T(128)} %get-tuple-element.157) | copy-start | bytes 772
  288.5 7.6 %copy-start.70 = (f32[64]{0:T(128)S(1)}, f32[64]{0:T(128)}, u32[]{:S(2)}) copy-start(f32[64]{0:T(128)} %get-tuple-element.42) | copy-start | bytes 772
  288.5 7.6 %copy-start.71 = (f32[64]{0:T(128)S(1)}, f32[64]{0:T(128)}, u32[]{:S(2)}) copy-start(f32[64]{0:T(128)} %get-tuple-element.97) | copy-start | bytes 772
  (38 other events, 267.7 us)
where the time goes:
time: 428 us; the launch traced here: 420 us
  other arithmetic  188 us (44%)
  blocking collectives  124 us (29%)
  starting transfers between devices  75.4 us (18%)
  local copies, waits for them, and re-layouts  21.3 us (5%)
  waiting for transfers between devices  7.75 us (2%)
    psum x1, blocking collectives, per_device(): lax.psum((partial_weight, bias_part, norm_scale_gradient, shift_grad, ker...  124 us
    reduce_sum x1, other arithmetic, apply_layer_norm(): spread = jnp.mean(center * center, axis=0, keepdims=True)  58.9 us
    reduce_sum x1, other arithmetic, apply_layer_norm(): center = values - jnp.mean(values, axis=0, keepdims=True)  31.6 us
    ppermute x4, starting transfers between devices, extended(): lax.ppermute(lax.slice_in_dim(block, block.shape[dim] - width, None, axis...  23.7 us
    reduce_sum x1, other arithmetic, per_device(): jnp.sum(normalized_gradient * centered_input, axis=(1, 2))  22.9 us
    unnamed x1, other arithmetic  22.4 us
    all_to_all x1, starting transfers between devices, per_device(): lax.all_to_all(embed_patches(file_pixels, patchify_weight, patchify_bias)...  19.6 us
    reduce_sum x4, other arithmetic, kernel_terms(): terms.append(jnp.sum(window * upstream, axis=(1, 2)))  19.4 us
  transfers between devices with their start and end apart: 10, of which 3 were waited for; matrix products, arithmetic and copies ran while one was open for 13% of the time, Pallas kernels for 0%

commit v1 on v0

--- a/solution.py
+++ b/solution.py
@@ -72,12 +72,20 @@
     height = cotangent.shape[1]
     breadth = cotangent.shape[2]
     factor = 1.0 / math.sqrt(height * lax.axis_size("rows") * breadth * lax.axis_size("cols"))
-    patch_embedding = lax.all_to_all(
-        embed_patches(file_pixels, patchify_weight, patchify_bias),
-        "cols",
-        split_axis=2,
-        concat_axis=1,
-        tiled=True,
+    patch_embedding = jnp.concatenate(
+        lax.all_to_all(
+            jnp.stack(
+                jnp.split(
+                    embed_patches(file_pixels, patchify_weight, patchify_bias),
+                    lax.axis_size("cols"),
+                    axis=2,
+                )
+            ),
+            "cols",
+            0,
+            0,
+        ),
+        axis=1,
     )
     centered_input, inverse_deviation = apply_layer_norm(patch_embedding)
     scale_factor = norm_gain[:, None, None]

time: 428 us -> 275 us (0.64); the launches traced: 420 us -> 275 us
  other arithmetic: 188 us -> 39.5 us
  starting transfers between devices: 75.4 us -> 62.9 us
  local copies, waits for them, and re-layouts: 21.3 us -> 31.6 us
    reduce_sum x1, other arithmetic: 58.9 us -> 0.19 us  [apply_layer_norm(): spread = jnp.mean(center * center, axis=0, keepdims=True)]
    reduce_sum x1, other arithmetic: 31.6 us -> 0.11 us  [apply_layer_norm(): center = values - jnp.mean(values, axis=0, keepdims=True)]
    unnamed x1 -> x0, other arithmetic: 22.4 us -> none
    ppermute x4, starting transfers between devices: 17.5 us -> 7.78 us  [extended(): lax.ppermute(lax.slice_in_dim(block, 0, width, axis=dim), axis, backward)]
    reduce_sum x4, other arithmetic: 19.4 us -> 10.1 us  [kernel_terms(): terms.append(jnp.sum(window * upstream, axis=(1, 2)))]
    unnamed x157 -> x75, local copies, waits for them, and re-layouts: 14.2 us -> 22.1 us
    convert_element_type x1, other arithmetic: 17.8 us -> 10.4 us  [per_device(): stem_output = (depthwise(padded, kernel, height, breadth) + kernel_offset...]
    concatenate x2, other arithmetic: 7.89 us -> 0.96 us  [extended(): block = jnp.concatenate([low, block, high], axis=dim)]
  transfers between devices with their start and end apart: 10 -> 10, of which waited for: 3 -> 4; matrix products, arithmetic and copies ran while one was open for 13% -> 11% of each run, Pallas kernels for 0% -> 0%
where the time goes in v1:
time: 275 us
  blocking collectives  128 us (47%)
  starting transfers between devices  62.9 us (23%)
  other arithmetic  39.5 us (14%)
  local copies, waits for them, and re-layouts  31.6 us (11%)
  waiting for transfers between devices  9.87 us (4%)
    psum x1, blocking collectives, per_device(): lax.psum((partial_weight, bias_part, norm_scale_gradient, shift_grad, ker...  128 us
    ppermute x4, starting transfers between devices, extended(): lax.ppermute(lax.slice_in_dim(block, block.shape[dim] - width, None, axis...  22.7 us
    unnamed x75, local copies, waits for them, and re-layouts  22.1 us
    all_to_all x1, starting transfers between devices, per_device(): lax.all_to_all(jnp.stack(jnp.split(embed_patches(file_pixels, patchify_we...  19.4 us
    reduce_sum x1, other arithmetic, per_device(): jnp.sum(normalized_gradient * centered_input, axis=(1, 2))  16.2 us
    all_to_all x1, starting transfers between devices, per_device(): lax.all_to_all(patch_gradient, 'cols', split_axis=1, concat_axis=2, tiled...  13.1 us
    convert_element_type x1, other arithmetic, per_device(): stem_output = (depthwise(padded, kernel, height, breadth) + kernel_offset...  10.4 us
    reduce_sum x4, other arithmetic, kernel_terms(): terms.append(jnp.sum(window * upstream, axis=(1, 2)))  10.1 us
  transfers between devices with their start and end apart: 10, of which 4 were waited for; matrix products, arithmetic and copies ran while one was open for 11% of the time, Pallas kernels for 0%

profile of v1, /device:TPU:1, one launch (start us, length us, event | category | flops | bytes accessed | tf_op | source)
XLA Modules:
  0.0 274.5 jit_solution(17821440734200651115)
XLA Ops:
  0.6 1.0 copy-done
  1.6 1.0 fusion.1
  2.7 0.6 constant_dynamic-update-slice_fusion.31
  3.3 0.6 constant_dynamic-update-slice_fusion.30
  3.9 0.6 constant_dynamic-update-slice_fusion.29
  4.5 0.6 constant_dynamic-update-slice_fusion.28
  5.1 0.6 constant_dynamic-update-slice_fusion.27
  5.7 0.6 constant_dynamic-update-slice_fusion.26
  6.3 0.6 constant_dynamic-update-slice_fusion.25
  7.0 0.6 constant_dynamic-update-slice_fusion.24
  7.6 0.6 constant_dynamic-update-slice_fusion.23
  8.8 0.6 constant_dynamic-update-slice_fusion.21
  10.6 0.6 constant_dynamic-update-slice_fusion.18
  13.7 0.6 constant_dynamic-update-slice_fusion.13
  15.5 0.6 constant_dynamic-update-slice_fusion.10
  17.3 0.6 constant_dynamic-update-slice_fusion.7
  18.6 0.6 constant_dynamic-update-slice_fusion.5
  20.4 0.6 constant_dynamic-update-slice_fusion.2
  22.2 19.4 %all-to-all-start = ((bf16[32,64,1,128]{3,1,2,0:T(8,128)(2,1)}), bf16[32,64,1,128]{3,1,2,0:T(8,128)(2,1)S(1)}, u32[]{:S(2)}, u32[]{:S(2)}) async-start(bf16[32,64,1,128]{3,1,2,0:T(8,128)(2,1)} %constant_dynamic-update-slice_fusion), calls=%async_computation | async-start | bytes 1048576 | tf_op jit(solution)/shard_map/all_to_all | solution.py:76
  41.7 3.1 %collective-permute-start.4 = (bf16[64,3,128]{2,0,1:T(8,128)(2,1)S(1)}, bf16[64,3,128]{2,0,1:T(8,128)(2,1)S(1)}, u32[]{:S(2)}, u32[]{:S(2)}) collective-permute-start(bf16[64,3,128]{2,0,1:T(8,128)(2,1)S(1)} %copy.105), channel_id=1, source_target_pairs={{0,32},{32,64},{64,96},{96,128},{128,160},{160,192},{192,224},{224... | collective-permute-start | bytes 147464 | tf_op jit(solution)/shard_map/ppermute | solution.py:16
  44.9 1.3 collective-permute-start.5
  46.8 3.1 %collective-permute-done.5 = bf16[64,3,128]{2,0,1:T(8,128)(2,1)S(1)} collective-permute-done((bf16[64,3,128]{2,0,1:T(8,128)(2,1)S(1)}, bf16[64,3,128]{2,0,1:T(8,128)(2,1)S(1)}, u32[]{:S(2)}, u32[]{:S(2)}) %collective-permute-start.5) | collective-permute-done | bytes 49184 | tf_op jit(solution)/shard_map/ppermute | solution.py:19
  50.0 1.3 fusion.240
  51.3 1.4 copy.37
  52.7 1.4 copy.40
  54.1 3.3 %collective-permute-start.7 = (bf16[64,38,3]{0,1,2:T(8,128)(2,1)S(1)}, bf16[64,38,3]{0,1,2:T(8,128)(2,1)S(1)}, u32[]{:S(2)}, u32[]{:S(2)}) collective-permute-start(bf16[64,38,3]{0,1,2:T(8,128)(2,1)S(1)} %copy.40), channel_id=1, source_target_pairs={{1,0},{2,1},{3,2},{4,3},{5,4},{6,5},{7,6},{8,7},{9,8},{10,9},{11,1... | collective-permute-start | bytes 43784 | tf_op jit(solution)/shard_map/ppermute | solution.py:19
  57.4 7.2 %collective-permute-start.6 = (bf16[64,38,3]{0,1,2:T(8,128)(2,1)S(1)}, bf16[64,38,3]{0,1,2:T(8,128)(2,1)S(1)}, u32[]{:S(2)}, u32[]{:S(2)}) collective-permute-start(bf16[64,38,3]{0,1,2:T(8,128)(2,1)S(1)} %copy.37), channel_id=1, source_target_pairs={{0,1},{1,2},{2,3},{3,4},{4,5},{5,6},{6,7},{7,8},{8,9},{9,10},{10,1... | collective-permute-start | bytes 43784 | tf_op jit(solution)/shard_map/ppermute | solution.py:16
  64.6 2.5 collective-permute-done.6
  67.1 1.1 copy.38
  68.3 0.7 collective-permute-done.7
  69.0 1.1 copy.41
  70.5 0.7 copy-done.2
  71.4 16.2 %fusion.188 = (f32[64]{0:T(128)}, f32[32,128]{1,0:T(8,128)S(1)}, f32[32,128]{1,0:T(8,128)S(1)}, f32[64]{0:T(128)}, f32[64,32,128]{2,0,1:T(8,128)S(1)}) fusion(bf16[32,64,1,128]{3,1,2,0:T(8,128)(2,1)S(1)} %all-to-all-done, f32[32,128]{1,0:T(8,128)S(1)} %add_rsqrt_fusion, f32[32,128]{1,0:T(8,128)S(1)} %broadcast_multiply_fusion.2, ...), kind=kLoop, calls=%fused_computation.324 | loop fusion | flops 74178432 | bytes 5973504 | tf_op jit(solution)/shard_map/reduce_sum | solution.py:106
  87.6 1.3 fusion.187
  89.0 4.9 %collective-permute-start = (bf16[64,3,128]{2,0,1:T(8,128)(2,1)S(1)}, bf16[64,3,128]{2,0,1:T(8,128)(2,1)S(1)}, u32[]{:S(2)}, u32[]{:S(2)}) collective-permute-start(bf16[64,3,128]{2,0,1:T(8,128)(2,1)S(1)} %get-tuple-element.108), channel_id=1, source_target_pairs={{0,32},{32,64},{64,96},{96,128},{128,160},{160,192},{192,224},{224... | collective-permute-start | bytes 147464 | tf_op jit(solution)/shard_map/ppermute | solution.py:16
  93.9 1.3 collective-permute-start.1
  95.2 3.5 %collective-permute-done.1 = bf16[64,3,128]{2,0,1:T(8,128)(2,1)S(1)} collective-permute-done((bf16[64,3,128]{2,0,1:T(8,128)(2,1)S(1)}, bf16[64,3,128]{2,0,1:T(8,128)(2,1)S(1)}, u32[]{:S(2)}, u32[]{:S(2)}) %collective-permute-start.1) | collective-permute-done | bytes 49184 | tf_op jit(solution)/shard_map/ppermute | solution.py:19
  99.4 7.4 %collective-permute-start.2 = (bf16[64,38,3]{0,1,2:T(8,128)(2,1)S(1)}, bf16[64,38,3]{0,1,2:T(8,128)(2,1)S(1)}, u32[]{:S(2)}, u32[]{:S(2)}) collective-permute-start(bf16[64,38,3]{0,1,2:T(8,128)(2,1)S(1)} %copy.30), channel_id=1, source_target_pairs={{0,1},{1,2},{2,3},{3,4},{4,5},{5,6},{6,7},{7,8},{8,9},{9,10},{10,1... | collective-permute-start | bytes 43784 | tf_op jit(solution)/shard_map/ppermute | solution.py:16
  107.2 1.9 collective-permute-start.3
  109.1 13.1 %all-to-all-start.1 = ((bf16[64,32,128]{2,0,1:T(8,128)(2,1)}), bf16[64,32,128]{2,0,1:T(8,128)(2,1)S(1)}, u32[]{:S(2)}, u32[]{:S(2)}) async-start(bf16[64,32,128]{2,0,1:T(8,128)(2,1)} %get-tuple-element.101), calls=%async_computation.1 | async-start | bytes 1048576 | tf_op jit(solution)/shard_map/all_to_all | solution.py:115
  123.1 0.9 maximum_maximum_fusion
  124.0 10.4 %add_convert_fusion = bf16[64,32,128]{2,0,1:T(8,128)(2,1)S(1)} fusion(bf16[64,32,128]{2,0,1:T(8,128)(2,1)S(1)} %get-tuple-element.102, bf16[64,3,128]{2,0,1:T(8,128)(2,1)S(1)} %collective-permute-done.1, bf16[64,3,128]{2,0,1:T(8,128)(2,1)S(1)} %collective-permute-done, f32[64]{0:T(128)S(1)} %copy-done.17, f32[64]{0:T(128)S(1)} %copy-done.12, ...), kind=kLoop, calls=%fused_computation.327 | loop fusion | flops 40370176 | bytes 23179776 | tf_op jit(solution)/shard_map/convert_element_type | solution.py:101
  134.4 1.1 copy.45
  135.6 0.7 fusion.102
  136.3 1.9 fusion.145
  138.2 3.6 %fusion.144 = (f32[64]{0:T(128)S(1)}, f32[64]{0:T(128)S(1)}, f32[64]{0:T(128)S(1)}, f32[64]{0:T(128)S(1)}, f32[64]{0:T(128)S(1)}, /*index=5*/f32[64]{0:T(128)S(1...) fusion(bf16[64,38,131]{2,0,1:T(8,128)(2,1)S(1)} %get-tuple-elem, ...), kind=kLoop, calls=%fused_computation.280 | loop fusion | flops 14678912 | bytes 9966080 | tf_op jit(solution)/shard_map/reduce_sum | solution.py:58
  141.8 3.8 %fusion.148 = (f32[64]{0:T(128)S(1)}, f32[64]{0:T(128)S(1)}, f32[64]{0:T(128)S(1)}, f32[64]{0:T(128)S(1)}, f32[64]{0:T(128)S(1)}, /*index=5*/f32[64]{0:T(128)S(1...) fusion(bf16[64,38,131]{2,0,1:T(8,128)(2,1)S(1)} %get-tuple-elem, ...), kind=kLoop, calls=%fused_computation.284 | loop fusion | flops 14678912 | bytes 9966080 | tf_op jit(solution)/shard_map/reduce_sum | solution.py:58
  146.4 128.2 %all-reduce = (f32[64,48]{0,1:T(8,128)}, f32[64]{0:T(128)}, f32[64]{0:T(128)}, f32[64]{0:T(128)}, f32[64,49]{0,1:T(8,128)}, /*index=5*/f32[64]{0:T(128)}) all-reduce(f32[64,48]{0,1:T(8,128)S(1)} %fusion.234, f32[64]{0:T(128)S(1)} %convert_reduce_fusion, f32[64]{0:T(128)S(1)} %copy-done.15, ...), channel_id=1, replica_groups=mesh['rows'=16,'cols'=32] {'rows','cols'}, use_global_device_ids=true, to_apply=%region_4.0 | all-reduce | flops 6464 | bytes 51712 | tf_op jit(solution)/shard_map/psum | solution.py:123
  (85 shorter events, 13.5 us)
Async XLA Ops:
  0.6 1.0 copy-start
  2.7 39.0 %copy-start.1 = (bf16[64,32,128]{2,1,0:T(8,128)(2,1)S(1)}, bf16[64,32,128]{2,1,0:T(8,128)(2,1)}, u32[]{:S(2)}) copy-start(bf16[64,32,128]{2,1,0:T(8,128)(2,1)} %param.15) | copy-start | bytes 1572868
  4.5 41.7 %copy-start.4 = (f32[64,49]{0,1:T(8,128)S(1)}, f32[64,49]{0,1:T(8,128)}, u32[]{:S(2)}) copy-start(f32[64,49]{0,1:T(8,128)} %param.13) | copy-start | bytes 37636
  22.2 47.9 %all-to-all-start = ((bf16[32,64,1,128]{3,1,2,0:T(8,128)(2,1)}), bf16[32,64,1,128]{3,1,2,0:T(8,128)(2,1)S(1)}, u32[]{:S(2)}, u32[]{:S(2)}) async-start(bf16[32,64,1,128]{3,1,2,0:T(8,128)(2,1)} %constant_dynamic-update-slice_fusion), calls=%async_computation | async-start | bytes 1048576 | tf_op jit(solution)/shard_map/all_to_all | solution.py:76
  41.7 4.6 %collective-permute-start.4 = (bf16[64,3,128]{2,0,1:T(8,128)(2,1)S(1)}, bf16[64,3,128]{2,0,1:T(8,128)(2,1)S(1)}, u32[]{:S(2)}, u32[]{:S(2)}) collective-permute-start(bf16[64,3,128]{2,0,1:T(8,128)(2,1)S(1)} %copy.105), channel_id=1, source_target_pairs={{0,32},{32,64},{64,96},{96,128},{128,160},{160,192},{192,224},{224... | collective-permute-start | bytes 147464 | tf_op jit(solution)/shard_map/ppermute | solution.py:16
  44.9 5.1 %collective-permute-start.5 = (bf16[64,3,128]{2,0,1:T(8,128)(2,1)S(1)}, bf16[64,3,128]{2,0,1:T(8,128)(2,1)S(1)}, u32[]{:S(2)}, u32[]{:S(2)}) collective-permute-start(bf16[64,3,128]{2,0,1:T(8,128)(2,1)S(1)} %copy.106), channel_id=1, source_target_pairs={{32,0},{64,32},{96,64},{128,96},{160,128},{192,160},{224,192},{256... | collective-permute-start | bytes 147464 | tf_op jit(solution)/shard_map/ppermute | solution.py:19
  46.2 24.2 %copy-start.5 = (f32[64]{0:T(128)}, f32[64]{0:T(128)S(1)}, u32[]{:S(2)}) copy-start(f32[64]{0:T(128)S(1)} %get-tuple-element.158) | copy-start | bytes 772
  46.2 24.2 %copy-start.7 = (f32[64]{0:T(128)}, f32[64]{0:T(128)S(1)}, u32[]{:S(2)}) copy-start(f32[64]{0:T(128)S(1)} %get-tuple-element.159) | copy-start | bytes 772
  46.3 24.2 %copy-start.9 = (f32[64]{0:T(128)}, f32[64]{0:T(128)S(1)}, u32[]{:S(2)}) copy-start(f32[64]{0:T(128)S(1)} %get-tuple-element.160) | copy-start | bytes 772
  46.3 24.2 %copy-start.11 = (f32[64]{0:T(128)}, f32[64]{0:T(128)S(1)}, u32[]{:S(2)}) copy-start(f32[64]{0:T(128)S(1)} %get-tuple-element.161) | copy-start | bytes 772
  46.3 24.2 %copy-start.13 = (f32[64]{0:T(128)}, f32[64]{0:T(128)S(1)}, u32[]{:S(2)}) copy-start(f32[64]{0:T(128)S(1)} %get-tuple-element.162) | copy-start | bytes 772
  51.3 13.3 %copy-start.18 = (f32[64]{0:T(128)S(1)}, f32[64]{0:T(128)}, u32[]{:S(2)}) copy-start(f32[64]{0:T(128)} %param.11) | copy-start | bytes 772
  54.1 14.9 %collective-permute-start.7 = (bf16[64,38,3]{0,1,2:T(8,128)(2,1)S(1)}, bf16[64,38,3]{0,1,2:T(8,128)(2,1)S(1)}, u32[]{:S(2)}, u32[]{:S(2)}) collective-permute-start(bf16[64,38,3]{0,1,2:T(8,128)(2,1)S(1)} %copy.40), channel_id=1, source_target_pairs={{1,0},{2,1},{3,2},{4,3},{5,4},{6,5},{7,6},{8,7},{9,8},{10,9},{11,1... | collective-permute-start | bytes 43784 | tf_op jit(solution)/shard_map/ppermute | solution.py:19
  57.4 9.7 %collective-permute-start.6 = (bf16[64,38,3]{0,1,2:T(8,128)(2,1)S(1)}, bf16[64,38,3]{0,1,2:T(8,128)(2,1)S(1)}, u32[]{:S(2)}, u32[]{:S(2)}) collective-permute-start(bf16[64,38,3]{0,1,2:T(8,128)(2,1)S(1)} %copy.37), channel_id=1, source_target_pairs={{0,1},{1,2},{2,3},{3,4},{4,5},{5,6},{6,7},{7,8},{8,9},{9,10},{10,1... | collective-permute-start | bytes 43784 | tf_op jit(solution)/shard_map/ppermute | solution.py:16
  70.1 1.1 copy-start.2
  70.1 1.3 copy-start.3
  71.4 16.2 %copy-start.19 = (f32[64]{0:T(128)S(1)}, f32[64]{0:T(128)}, u32[]{:S(2)}) copy-start(f32[64]{0:T(128)} %param.12) | copy-start | bytes 772
  89.0 6.2 %collective-permute-start = (bf16[64,3,128]{2,0,1:T(8,128)(2,1)S(1)}, bf16[64,3,128]{2,0,1:T(8,128)(2,1)S(1)}, u32[]{:S(2)}, u32[]{:S(2)}) collective-permute-start(bf16[64,3,128]{2,0,1:T(8,128)(2,1)S(1)} %get-tuple-element.108), channel_id=1, source_target_pairs={{0,32},{32,64},{64,96},{96,128},{128,160},{160,192},{192,224},{224... | collective-permute-start | bytes 147464 | tf_op jit(solution)/shard_map/ppermute | solution.py:16
  93.9 4.8 %collective-permute-start.1 = (bf16[64,3,128]{2,0,1:T(8,128)(2,1)S(1)}, bf16[64,3,128]{2,0,1:T(8,128)(2,1)S(1)}, u32[]{:S(2)}, u32[]{:S(2)}) collective-permute-start(bf16[64,3,128]{2,0,1:T(8,128)(2,1)S(1)} %get-tuple-element.109), channel_id=1, source_target_pairs={{32,0},{64,32},{96,64},{128,96},{160,128},{192,160},{224,192},{256... | collective-permute-start | bytes 147464 | tf_op jit(solution)/shard_map/ppermute | solution.py:19
  99.4 22.8 %collective-permute-start.2 = (bf16[64,38,3]{0,1,2:T(8,128)(2,1)S(1)}, bf16[64,38,3]{0,1,2:T(8,128)(2,1)S(1)}, u32[]{:S(2)}, u32[]{:S(2)}) collective-permute-start(bf16[64,38,3]{0,1,2:T(8,128)(2,1)S(1)} %copy.30), channel_id=1, source_target_pairs={{0,1},{1,2},{2,3},{3,4},{4,5},{5,6},{6,7},{7,8},{8,9},{9,10},{10,1... | collective-permute-start | bytes 43784 | tf_op jit(solution)/shard_map/ppermute | solution.py:16
  107.2 15.4 %collective-permute-start.3 = (bf16[64,38,3]{0,1,2:T(8,128)(2,1)S(1)}, bf16[64,38,3]{0,1,2:T(8,128)(2,1)S(1)}, u32[]{:S(2)}, u32[]{:S(2)}) collective-permute-start(bf16[64,38,3]{0,1,2:T(8,128)(2,1)S(1)} %copy.32), channel_id=1, source_target_pairs={{1,0},{2,1},{3,2},{4,3},{5,4},{6,5},{7,6},{8,7},{9,8},{10,9},{11,1... | collective-permute-start | bytes 43784 | tf_op jit(solution)/shard_map/ppermute | solution.py:19
  109.1 36.8 %all-to-all-start.1 = ((bf16[64,32,128]{2,0,1:T(8,128)(2,1)}), bf16[64,32,128]{2,0,1:T(8,128)(2,1)S(1)}, u32[]{:S(2)}, u32[]{:S(2)}) async-start(bf16[64,32,128]{2,0,1:T(8,128)(2,1)} %get-tuple-element.101), calls=%async_computation.1 | async-start | bytes 1048576 | tf_op jit(solution)/shard_map/all_to_all | solution.py:115
  123.0 1.0 copy-start.6
  123.0 1.0 copy-start.8
  123.0 1.0 copy-start.10
  123.0 1.0 copy-start.12
  123.0 1.0 copy-start.14
  123.1 1.0 copy-start.17
  145.7 0.7 copy-start.15
  145.7 0.7 copy-start.16
